TPU v7x, 32 devices: a whole 2x2x4 slice. The times are simulated.
32 devices in a mesh: sec: 2 (over core), elem: 16 (over z, y, x).
Axes of the slice: x: 2, y: 2, z: 4, core: 2. Of those that a mesh axis runs over, the one named last changes fastest.
Arguments:
- fields: float32 [2, 320, 16384], P('sec', None, 'elem'), may hold values from -6 to 6
- jacobian: float32 [2, 16384], P('sec', 'elem'), may hold values from 0.25 to 2.5
- face_links: int32 [2, 6, 16384], P('sec', None, 'elem'), may hold values from 0 to 1535, as said below
- volume_matrix: float32 [2, 320, 320], P('sec'), may hold values from -0.3125 to 0.3125
- face_matrices: float32 [2, 6, 320, 320], P('sec'), may hold values from -0.3125 to 0.3125
- patterns: float32 [4, 64, 64], replicated, may hold values from 0 to 0.03125
- donor_index: int32 [2, 2048], P('sec', 'elem'), may hold values from 0 to 1023
- pattern_index: int32 [2, 2048], P('sec', 'elem'), may hold values from 0 to 3
- receivers: int32 [2, 2048], P('sec', 'elem'), may hold values from -1 to 1023, as said below
Outputs:
- advanced: float32 [2, 320, 16384], P('sec', None, 'elem')
Inputs may be any that keep to these rules, and one draw needn't show every extreme that they name: face_links[s, f, g] counts from the lowest rim element of the device holding element g; index 256 is that device's first own element. receivers holds on each device 8 slots for each device of the other section, source-major; -1 marks an empty slot, other entries on one device are distinct; in every draw some device gets 8 blocks from every device of the other section.
All inputs are finite; a program needn't handle non-finite values.
Results may differ from a plain program's by a relative error of at most 0.0001.
Values sent between devices are 32-bit elements; how exact they have to be, the bound alone decides.
A program may use at most 64 MiB of HBM per device.

v0:
```python
import functools

import jax
import jax.numpy as jnp
from jax import lax
from jax.experimental import pallas as pl
from jax.experimental.pallas import tpu as pltpu
from jax.sharding import PartitionSpec as P

NODES = 64
HALO = 256
LANES = 128
ROWS = 4
DEPTH = 384
PARTS = DEPTH // LANES
STEP = 0.25
MESH = pl.DeviceIdType.MESH
F32 = jnp.float32
BF16 = jnp.bfloat16


def split(value):
    high = value.astype(BF16)
    return high, (value - high.astype(F32)).astype(BF16)


def kernel(
    n,
    links,
    scale,
    donors,
    select,
    fields,
    volume,
    faces,
    patterns,
    choose,
    out,
    table,
    landed,
    first,
    second,
    donated,
    outgoing,
    packed,
    rims,
    operand,
    weights,
    padded,
    own,
    mapped,
    block_send,
    block_recv,
    rim_send,
    rim_recv,
):
    sec, me = lax.axis_index("sec"), lax.axis_index("elem")
    other = 1 - sec
    elements = fields.shape[1]
    slots = donors.shape[1]
    per_device = slots // n
    block = per_device * ROWS
    components = fields.shape[0]
    tail = components - 2 * LANES

    barrier = pltpu.get_barrier_semaphore()
    for j in range(n):
        pl.semaphore_signal(barrier, inc=1, device_id=(other, j), device_id_type=MESH)

    @pl.when(me > 0)
    def _():
        pl.semaphore_signal(barrier, inc=1, device_id=(sec, me - 1), device_id_type=MESH)

    @pl.when(me < n - 1)
    def _():
        pl.semaphore_signal(barrier, inc=1, device_id=(sec, me + 1), device_id_type=MESH)

    for c in range(elements // LANES):
        for j in range(PARTS):
            if j < 2:
                piece = fields[j * LANES : (j + 1) * LANES, c * LANES : (c + 1) * LANES]
            else:
                piece = jnp.concatenate(
                    [
                        fields[2 * LANES : components, c * LANES : (c + 1) * LANES],
                        jnp.zeros((LANES - tail, LANES), F32),
                    ],
                    axis=0,
                )
            table[pl.ds(c * LANES * ROWS + j, LANES, stride=ROWS), :] = jnp.transpose(piece)
        table[pl.ds(c * LANES * ROWS + 3, LANES, stride=ROWS), :] = jnp.zeros((LANES, LANES), F32)

    def prepare_weights():
        padded[...] = jnp.zeros_like(padded)
        for f in range(7):
            padded[0:components, 0:components] = volume[...] if f == 6 else faces[f]
            for k in range(PARTS):
                strip = jnp.transpose(padded[:, k * LANES : (k + 1) * LANES])
                high, low = split(strip)
                pair, lanes = f // 2, slice(f % 2 * DEPTH, f % 2 * DEPTH + DEPTH)
                if k < 2:
                    places = ((k * LANES, high), ((2 + k) * LANES, high), ((4 + k) * LANES, low))
                    for row, value in places:
                        weights[pair, row : row + LANES, lanes] = value
                else:
                    ends = (high[:tail], high[:tail], low[:tail], jnp.zeros_like(low[:tail]))
                    for m, value in enumerate(ends):
                        row = 6 * LANES + m * tail
                        weights[pair, row : row + tail, lanes] = value

    def rim_copy(stage, side):
        target = me - 1 if side == 0 else me + 1
        return pltpu.make_async_remote_copy(
            src_ref=packed.at[side],
            dst_ref=rims.at[stage, 1 - side],
            send_sem=rim_send.at[stage, side],
            recv_sem=rim_recv.at[stage, 1 - side],
            device_id=(sec, target),
            device_id_type=MESH,
        )

    def to_operand(row, count, parts):
        rows = pl.ds(row, count)
        for k in range(2):
            high, low = split(parts[k])
            operand[rows, k * LANES : (k + 1) * LANES] = high
            operand[rows, (2 + k) * LANES : (3 + k) * LANES] = low
            operand[rows, (4 + k) * LANES : (5 + k) * LANES] = high
        high, low = split(parts[2])
        both = high.astype(F32) + pltpu.roll(low.astype(F32), tail, 1)
        operand[rows, 6 * LANES : 7 * LANES] = both.astype(BF16)
        operand[rows, 7 * LANES : 8 * LANES] = high

    def face_products(row):
        def body(pair, carry):
            y = jnp.dot(
                operand[pl.ds(pl.multiple_of(row, HALO), HALO), :],
                weights[pair],
                preferred_element_type=F32,
            )
            for half in range(2):
                for k in range(PARTS):
                    at = half * DEPTH + k * LANES
                    mapped[pair * 2 + half, pl.ds(row * ROWS + k, HALO, stride=ROWS), :] = y[:, at : at + LANES]
            return carry

        lax.fori_loop(0, 3, body, 0)

    for stage in range(2):
        state = first if stage == 0 else second

        def donate(i, carry):
            for u in range(8):
                b = i * 8 + u
                row = donors[0, b] * ROWS
                donated[pl.ds(pl.multiple_of(b * ROWS, ROWS), ROWS), :] = table[pl.ds(row, ROWS), :]
            return carry

        lax.fori_loop(0, slots // 8, donate, 0)
        values = donated[...]
        shape = (slots * ROWS, slots)
        mine = lax.broadcasted_iota(jnp.int32, shape, 0) // ROWS == lax.broadcasted_iota(jnp.int32, shape, 1)
        kinds = jnp.sum(jnp.where(mine, choose[...].astype(F32), 0.0), axis=1, keepdims=True)
        result = jnp.zeros((slots * ROWS, LANES), F32)
        for p in range(patterns.shape[0]):
            one = patterns[p]
            none = jnp.zeros_like(one)
            twice = jnp.concatenate(
                [jnp.concatenate([one, none], axis=1), jnp.concatenate([none, one], axis=1)], axis=0
            )
            moved = lax.dot_general(
                values,
                twice,
                (((1,), (1,)), ((), ())),
                precision=lax.Precision.HIGHEST,
                preferred_element_type=F32,
            )
            result = jnp.where(kinds == float(p), moved, result)
        outgoing[...] = result

        if stage == 0:
            heard = n + (me > 0).astype(jnp.int32) + (me < n - 1).astype(jnp.int32)
            pl.semaphore_wait(barrier, heard)

        def block_copy(j):
            return pltpu.make_async_remote_copy(
                src_ref=outgoing.at[pl.ds(pl.multiple_of(j * block, block), block)],
                dst_ref=landed.at[stage, pl.ds(pl.multiple_of(me * block, block), block)],
                send_sem=block_send.at[stage, j],
                recv_sem=block_recv.at[stage, me],
                device_id=(other, j),
                device_id_type=MESH,
            )

        def arrived(j):
            return pltpu.make_async_remote_copy(
                src_ref=outgoing.at[pl.ds(pl.multiple_of(j * block, block), block)],
                dst_ref=landed.at[stage, pl.ds(pl.multiple_of(j * block, block), block)],
                send_sem=block_send.at[stage, j],
                recv_sem=block_recv.at[stage, j],
                device_id=(other, j),
                device_id_type=MESH,
            )

        for j in range(n):
            block_copy(j).start()
        if stage == 0:
            prepare_weights()
        for j in range(n):
            arrived(j).wait_recv()
        table[elements * ROWS :, :] = landed[stage]

        def pick(i, carry):
            for u in range(8):
                g = i * 8 + u
                row = select[0, g] * ROWS
                state[pl.ds(pl.multiple_of(g * ROWS, ROWS), ROWS), :] = table[pl.ds(row, ROWS), :]
            return carry

        def rim_parts(row):
            return [state[pl.ds(row * ROWS + k, HALO, stride=ROWS), :] for k in range(PARTS)]

        for side, begin in ((0, 0), (1, elements - HALO)):
            lax.fori_loop(begin // 8, (begin + HALO) // 8, pick, 0)
            parts = rim_parts(begin)
            packed[side, 0:HALO, :] = parts[0]
            packed[side, HALO : 2 * HALO, :] = parts[1]
            lower, upper = parts[2][: HALO // 2], parts[2][HALO // 2 :]
            packed[side, 2 * HALO :, :] = lower + pltpu.roll(upper, tail, 1)

            @pl.when(me > 0 if side == 0 else me < n - 1)
            def _():
                rim_copy(stage, side).start()

            to_operand(HALO + begin, HALO, parts)
        lax.fori_loop(HALO // 8, (elements - HALO) // 8, pick, 0)
        for c in range(1, elements // HALO - 1):
            to_operand(HALO + c * HALO, HALO, rim_parts(c * HALO))

        def own_products(c, carry):
            row = HALO + c * HALO
            face_products(row)
            y = jnp.dot(
                operand[pl.ds(pl.multiple_of(row, HALO), HALO), :],
                weights[3, :, 0:DEPTH],
                preferred_element_type=F32,
            )
            for k in range(PARTS):
                own[pl.ds(c * HALO * ROWS + k, HALO, stride=ROWS), :] = y[:, k * LANES : (k + 1) * LANES]
            return carry

        lax.fori_loop(0, elements // HALO, own_products, 0)

        for side in (1, 0):
            row = 0 if side == 0 else HALO + elements
            inside = me > 0 if side == 0 else me < n - 1

            @pl.when(inside)
            def _():
                rim_copy(stage, 1 - side).wait_recv()
                folded = rims[stage, side, 2 * HALO :, :]
                lane = lax.broadcasted_iota(jnp.int32, folded.shape, 1)
                lower = jnp.where(lane < tail, folded, 0.0)
                upper = jnp.where(lane < tail, pltpu.roll(folded, LANES - tail, 1), 0.0)
                last = jnp.concatenate([lower, upper], axis=0)
                to_operand(row, HALO, [rims[stage, side, 0:HALO, :], rims[stage, side, HALO : 2 * HALO, :], last])
                face_products(row)

            @pl.when(jnp.logical_not(inside))
            def _():
                for f in range(6):
                    mapped[f, row * ROWS : (row + HALO) * ROWS, :] = jnp.zeros((HALO * ROWS, LANES), F32)

        def advance(i, carry):
            for u in range(8):
                g = i * 8 + u
                here = pl.ds(pl.multiple_of(g * ROWS, ROWS), ROWS)
                total = own[here, :]
                for f in range(6):
                    row = links[f, 0, g] * ROWS
                    total = total + mapped[f, pl.ds(row, ROWS), :]
                stepped = state[here, :] + scale[0, g] * (STEP * total)
                if stage == 0:
                    table[here, :] = stepped
                else:
                    table[here, :] = 0.5 * first[here, :] + 0.5 * stepped
            return carry

        lax.fori_loop(0, elements // 8, advance, 0)
        for j in range(n):
            block_copy(j).wait_send()
        for side in range(2):

            @pl.when(me > 0 if side == 0 else me < n - 1)
            def _():
                rim_copy(stage, side).wait_send()

    for c in range(elements // LANES):
        for j in range(PARTS):
            piece = jnp.transpose(table[pl.ds(c * LANES * ROWS + j, LANES, stride=ROWS), :])
            high = min((j + 1) * LANES, components)
            out[j * LANES : high, c * LANES : (c + 1) * LANES] = piece[: high - j * LANES]


def local(
    n,
    fields,
    jacobian,
    face_links,
    volume_matrix,
    face_matrices,
    patterns,
    donor_index,
    pattern_index,
    receivers,
):
    components, elements = fields.shape[1:]
    slots = donor_index.shape[1]
    slot = jnp.arange(slots, dtype=jnp.int32)
    hit = receivers[0][None, :] == jnp.arange(elements, dtype=jnp.int32)[:, None]
    found = jnp.max(jnp.where(hit, slot[None, :], -1), axis=1)
    index = jnp.arange(elements, dtype=jnp.int32)
    select = jnp.where(found >= 0, elements + found, index)[None]
    smem = pl.BlockSpec(memory_space=pltpu.SMEM)
    vmem = pl.BlockSpec(memory_space=pltpu.VMEM)
    wide = elements + 2 * HALO
    result = pl.pallas_call(
        functools.partial(kernel, n),
        out_shape=jax.ShapeDtypeStruct((components, elements), F32),
        in_specs=[smem] * 4 + [vmem] * 5,
        out_specs=vmem,
        scratch_shapes=[
            pltpu.VMEM(((elements + slots) * ROWS, LANES), F32),
            pltpu.VMEM((2, slots * ROWS, LANES), F32),
            pltpu.VMEM((elements * ROWS, LANES), F32),
            pltpu.VMEM((elements * ROWS, LANES), F32),
            pltpu.VMEM((slots * ROWS, LANES), F32),
            pltpu.VMEM((slots * ROWS, LANES), F32),
            pltpu.VMEM((2, 5 * HALO // 2, LANES), F32),
            pltpu.VMEM((2, 2, 5 * HALO // 2, LANES), F32),
            pltpu.VMEM((wide, 8 * LANES), BF16),
            pltpu.VMEM((4, 8 * LANES, 2 * DEPTH), BF16),
            pltpu.VMEM((DEPTH, DEPTH), F32),
            pltpu.VMEM((elements * ROWS, LANES), F32),
            pltpu.VMEM((6, wide * ROWS, LANES), F32),
            pltpu.SemaphoreType.DMA((2, n)),
            pltpu.SemaphoreType.DMA((2, n)),
            pltpu.SemaphoreType.DMA((2, 2)),
            pltpu.SemaphoreType.DMA((2, 2)),
        ],
        compiler_params=pltpu.CompilerParams(
            collective_id=0, has_side_effects=True, vmem_limit_bytes=62 * 1024 * 1024
        ),
    )(
        jnp.transpose(face_links, (1, 0, 2)),
        jacobian,
        donor_index,
        select,
        fields[0],
        volume_matrix[0],
        face_matrices[0],
        patterns,
        pattern_index,
    )
    return result[None]


def solution(mesh):
    return jax.shard_map(
        functools.partial(local, mesh.shape["elem"]),
        mesh=mesh,
        in_specs=(
            P("sec", None, "elem"),
            P("sec", "elem"),
            P("sec", None, "elem"),
            P("sec", None, None),
            P("sec", None, None, None),
            P(),
            P("sec", "elem"),
            P("sec", "elem"),
            P("sec", "elem"),
        ),
        out_specs=P("sec", None, "elem"),
        check_vma=False,
    )
```

profile of v0, /device:TPU:13, one launch (start us, length us, event | category | flops | bytes accessed | tf_op | source)
XLA Modules:
  0.0 88.3 jit_solution(17625373561457566911)
XLA Ops:
  0.0 0.9 select_reduce_fusion
  0.9 0.6 reshape_select_fusion.select
  1.5 84.3 %shard_map.91 = f32[320,1024]{1,0:T(8,128)} custom-call(s32[6,1,1024]{2,1,0:T(1,128)} %bitcast.11, f32[1,1024]{1,0:T(1,128)} %scale.1, s32[1,128]{1,0:T(1,128)} %donors.1, s32[1,1024]{1,0:T(1,128)} %reshape_select_fusion.select, f32[320,1024]{1,0:T(8,128)} %bitcast.9, f32[320,320]{1,0:T(8,128)} %bitcast.10, f32[6,320,320]{2,1,0:T(8,128)} %bitcast.8, ...), custom_call_target="tpu_custom_call" | custom-call | tf_op jit(solution)/shard_map/pallas_call | solution.py:327
  85.8 2.5 %copy.11 = f32[1,320,1024]{2,1,0:T(8,128)} copy(f32[1,320,1024]{2,1,0:T(8,128)} %bitcast.7) | data formatting | bytes 2621440
  (2 shorter events, 0.0 us)
where the time goes:
time: 88.5 us; the launch traced here: 88.3 us
  Pallas kernels  84.3 us (95%)
  local copies, waits for them, and re-layouts  2.52 us (3%)
  other arithmetic  1.47 us (2%)
    pallas_call x1, Pallas kernels, local(): pl.pallas_call(functools.partial(kernel, n), out_shape=jax.ShapeDtypeStru...  84.3 us
    unnamed x1, local copies, waits for them, and re-layouts  2.52 us

commit v1 on v0

v1 whole, which is shorter than its diff:
```python
import functools

import jax
import jax.numpy as jnp
from jax import lax
from jax.experimental import pallas as pl
from jax.experimental.pallas import tpu as pltpu
from jax.sharding import PartitionSpec as P

HALO = 256
LANES = 128
CHUNK = 256
ROWS = 5
FACES = 6
STEP = 0.25
MESH = pl.DeviceIdType.MESH
F32 = jnp.float32
BF16 = jnp.bfloat16


def split(value):
    high = value.astype(BF16)
    return high, (value - high.astype(F32)).astype(BF16)


def cross(a, b):
    return lax.dot_general(a, b, (((1,), (1,)), ((), ())), preferred_element_type=F32)


def iota(shape, dim):
    return lax.broadcasted_iota(jnp.int32, shape, dim)


def column(row):
    return jnp.transpose(jnp.broadcast_to(row.astype(F32), (LANES, LANES))).astype(jnp.int32)


def kernel(
    n,
    index,
    fields,
    jacobian,
    links,
    donors,
    choose,
    receivers,
    patterns,
    volume_hbm,
    faces_hbm,
    out,
    volume,
    faces,
    first,
    state,
    total,
    halves,
    give,
    twice,
    mixed,
    donated,
    outgoing,
    landed,
    take,
    hit,
    table,
    gathered,
    even,
    odd,
    weights,
    rims,
    rim_operand,
    made_high,
    made_low,
    onehot,
    block_send,
    block_recv,
    rim_send,
    rim_recv,
    load,
):
    sec, me = lax.axis_index("sec"), lax.axis_index("elem")
    other = 1 - sec
    components, elements = fields.shape
    slots = donors.shape[1]
    per_device = slots // n
    rows = 2 * per_device + per_device // 2
    tail = components - 2 * LANES
    width = 8 * LANES
    half = HALO // 2

    barrier = pltpu.get_barrier_semaphore()
    for j in range(n):
        pl.semaphore_signal(barrier, inc=1, device_id=(other, j), device_id_type=MESH)

    @pl.when(me > 0)
    def _():
        pl.semaphore_signal(barrier, inc=1, device_id=(sec, me - 1), device_id_type=MESH)

    @pl.when(me < n - 1)
    def _():
        pl.semaphore_signal(barrier, inc=1, device_id=(sec, me + 1), device_id_type=MESH)

    volume_copy = pltpu.make_async_copy(volume_hbm, volume, load.at[0])
    faces_copy = pltpu.make_async_copy(faces_hbm, faces, load.at[1])
    volume_copy.start()
    faces_copy.start()

    for b in range(slots // LANES):
        rows_b = slice(b * LANES, (b + 1) * LANES)
        donor = column(donors[:, rows_b])
        for t in range(elements // LANES):
            lane = iota((LANES, LANES), 1) + t * LANES
            one = jnp.where(donor == lane, 1.0, 0.0).astype(BF16)
            give[rows_b, t * LANES : (t + 1) * LANES] = one
            give[rows_b, elements + t * LANES : elements + (t + 1) * LANES] = one
    kinds = [column(choose[:, b * LANES : (b + 1) * LANES]) for b in range(slots // LANES)]
    count = patterns.shape[0]
    for p in range(count):
        one = patterns[p]
        none = jnp.zeros_like(one)
        both = jnp.concatenate(
            [jnp.concatenate([one, none], axis=1), jnp.concatenate([none, one], axis=1)], axis=0
        )
        high, low = split(both)
        for part, value in enumerate((high, high, low)):
            at = (part * count + p) * LANES
            twice[:, at : at + LANES] = value

    def prepare_receivers():
        for t in range(elements // LANES):
            lane = iota((LANES, LANES), 1) + t * LANES
            here = slice(t * LANES, (t + 1) * LANES)
            seen = jnp.zeros((1, LANES), F32)
            for b in range(slots // LANES):
                one = jnp.where(column(receivers[:, b * LANES : (b + 1) * LANES]) == lane, 1.0, 0.0)
                seen = seen + jnp.sum(one, axis=0, keepdims=True)
                take[b * LANES : (b + 1) * LANES, here] = one.astype(BF16)
                take[slots + b * LANES : slots + (b + 1) * LANES, here] = one.astype(BF16)
            hit[:, here] = seen

    def prepare_weights():
        volume_copy.wait()
        faces_copy.wait()
        for f in range(FACES + 1):
            matrix = volume if f == FACES else faces.at[f]
            high, low = split(matrix[:, 0 : 2 * LANES])
            ends = matrix[:, 2 * LANES : components]
            end_high, end_low = split(jnp.concatenate([ends, ends], axis=1))
            lane = iota(end_low.shape, 1)
            end_low = jnp.where(lane < tail, end_low.astype(F32), 0.0).astype(BF16)
            at = f * width
            weights[:, at : at + 2 * LANES] = high
            weights[:, at + 2 * LANES : at + 4 * LANES] = high
            weights[:, at + 4 * LANES : at + 6 * LANES] = low
            weights[:, at + 6 * LANES : at + 7 * LANES] = end_high
            weights[:, at + 7 * LANES : at + 8 * LANES] = end_low

    def prepare_onehot():
        def body(f, carry):
            for h in range(2):
                for side in range(2):
                    begin = side * (HALO + elements) + h * half
                    for t in range(elements // CHUNK):
                        here = slice(t * CHUNK, (t + 1) * CHUNK)
                        row = links[pl.ds(f, 1), here]
                        one = jnp.where(row == iota((half, CHUNK), 0) + begin, 1.0, 0.0)
                        at = pl.multiple_of((h * FACES + f) * HALO + side * half, half)
                        onehot[pl.ds(at, half), here] = one.astype(BF16)
            return carry

        lax.fori_loop(0, FACES, body, 0)

    def rim_copy(stage, source, side, h):
        target = me - 1 if side == 0 else me + 1
        begin = h * half if side == 0 else elements - HALO + h * half
        return pltpu.make_async_remote_copy(
            src_ref=source.at[:, pl.ds(begin, half)],
            dst_ref=rims.at[stage, h, :, pl.ds((1 - side) * half, half)],
            send_sem=rim_send.at[stage, side, h],
            recv_sem=rim_recv.at[stage, 1 - side, h],
            device_id=(sec, target),
            device_id_type=MESH,
        )

    for stage in range(2):
        source = fields if stage == 0 else out
        patched = first if stage == 0 else state

        high, low = split(source[...])
        halves[:, 0:elements] = high
        halves[:, elements:] = low
        donated[:, 0:components] = cross(give[...], halves[...])
        for b in range(slots // LANES):
            for k in range(3):
                piece = donated[b * LANES : (b + 1) * LANES, k * LANES : (k + 1) * LANES]
                if k == 2:
                    piece = jnp.where(iota(piece.shape, 1) < tail, piece, 0.0)
                high = piece.astype(BF16).astype(F32)
                for p in range(count):
                    mask = kinds[b] == p
                    big = jnp.where(mask, high, 0.0).astype(BF16)
                    small = jnp.where(mask, piece - high, 0.0).astype(BF16)
                    row = k * slots + b * LANES
                    for part, value in enumerate((big, small, big)):
                        at = (part * count + p) * LANES
                        mixed[row : row + LANES, at : at + LANES] = value
        result = cross(mixed[...], twice[...])
        quarter = per_device // 2
        for j in range(n):
            at, slot = j * rows, j * per_device
            outgoing[at : at + per_device, :] = result[slot : slot + per_device]
            outgoing[at + per_device : at + 2 * per_device, :] = result[slots + slot : slots + slot + per_device]
            ends = result[2 * slots + slot : 2 * slots + slot + per_device]
            outgoing[at + 2 * per_device : at + rows, :] = ends[:quarter] + pltpu.roll(ends, tail, 1)[quarter:]

        if stage == 0:
            heard = n + (me > 0).astype(jnp.int32) + (me < n - 1).astype(jnp.int32)
            pl.semaphore_wait(barrier, heard)

        def block_copy(j):
            return pltpu.make_async_remote_copy(
                src_ref=outgoing.at[pl.ds(j * rows, rows)],
                dst_ref=landed.at[stage, pl.ds(me * rows, rows)],
                send_sem=block_send.at[stage, j],
                recv_sem=block_recv.at[stage, me],
                device_id=(other, j),
                device_id_type=MESH,
            )

        def arrived(j):
            return pltpu.make_async_remote_copy(
                src_ref=outgoing.at[pl.ds(j * rows, rows)],
                dst_ref=landed.at[stage, pl.ds(j * rows, rows)],
                send_sem=block_send.at[stage, j],
                recv_sem=block_recv.at[stage, j],
                device_id=(other, j),
                device_id_type=MESH,
            )

        for j in range(n):
            block_copy(j).start()
        if stage == 0:
            prepare_receivers()
            prepare_weights()
        for j in range(n):
            arrived(j).wait_recv()

        for b in range(slots // LANES):
            pieces = [[], [], []]
            for j in range(b * LANES // per_device, (b + 1) * LANES // per_device):
                at = j * rows
                pieces[0].append(landed[stage, at : at + per_device, :])
                pieces[1].append(landed[stage, at + per_device : at + 2 * per_device, :])
                ends = landed[stage, at + 2 * per_device : at + rows, :]
                pieces[2].append(jnp.concatenate([ends, pltpu.roll(ends, tail, 1)], axis=0))
            for k in range(3):
                count_k = LANES if k < 2 else tail
                high, low = split(jnp.transpose(jnp.concatenate(pieces[k], axis=0))[:count_k])
                here = slice(k * LANES, k * LANES + count_k)
                mixed_rows = halves
                mixed_rows[here, b * LANES : (b + 1) * LANES] = high
                mixed_rows[here, slots + b * LANES : slots + (b + 1) * LANES] = low
        chunks = elements // CHUNK
        for c in [0, chunks - 1] + list(range(1, chunks - 1)):
            here = slice(c * CHUNK, (c + 1) * CHUNK)
            moved = jnp.dot(halves[:, 0 : 2 * slots], take[:, here], preferred_element_type=F32)
            patched[:, here] = jnp.where(hit[:, here] > 0.5, moved, source[:, here])
            for side in range(2):
                if c == (0 if side == 0 else chunks - 1):

                    @pl.when(me > 0 if side == 0 else me < n - 1)
                    def _():
                        for h in range(2):
                            rim_copy(stage, patched, side, h).start()

        for t in range(elements // LANES):
            here = slice(t * LANES, (t + 1) * LANES)
            at = t * LANES * ROWS
            for k in range(2):
                piece = jnp.transpose(patched[k * LANES : (k + 1) * LANES, here])
                high = piece.astype(BF16).astype(F32)
                table[pl.ds(at + k, LANES, stride=ROWS), :] = high
                table[pl.ds(at + 2 + k, LANES, stride=ROWS), :] = piece - high
            ends = patched[2 * LANES : components, here]
            high = ends.astype(BF16).astype(F32)
            table[pl.ds(at + 4, LANES, stride=ROWS), :] = jnp.transpose(
                jnp.concatenate([high, ends - high], axis=0)
            )
        table[elements * ROWS :, :] = jnp.zeros((8, LANES), F32)
        if stage == 0:
            prepare_onehot()

        def to_operand(source_ref, target, f):
            for k in range(ROWS):
                target[f * ROWS + k] = source_ref[pl.ds(k, CHUNK, stride=ROWS), :].astype(BF16)

        def gather(c, target):
            for f in range(FACES):
                where = gathered.at[f]
                for e in range(CHUNK):
                    row = index[f * elements + c * CHUNK + e]
                    where[e * ROWS : (e + 1) * ROWS, :] = table[pl.ds(row, ROWS), :]
                to_operand(where, target, f)
            size = CHUNK * ROWS
            to_operand(table.at[pl.ds(c * size, size)], target, FACES)

        def contract(c, target):
            parts = []
            for f in range(FACES + 1):
                parts += [target[f * ROWS + k] for k in (0, 1, 2, 3, 0, 1, 4, 4)]
            total[c] = cross(weights[...], jnp.concatenate(parts, axis=1))

        gather(0, even)

        def own(i, carry):
            gather(2 * i + 1, odd)
            contract(2 * i, even)
            gather(lax.rem(2 * i + 2, chunks), even)
            contract(2 * i + 1, odd)
            return carry

        lax.fori_loop(0, chunks // 2, own, 0)

        for h in range(2):
            for side in range(2):
                inside = me > 0 if side == 0 else me < n - 1
                where = rims.at[stage, h, :, pl.ds(side * half, half)]

                @pl.when(inside)
                def _():
                    rim_copy(stage, patched, 1 - side, h).wait_recv()

                @pl.when(jnp.logical_not(inside))
                def _():
                    where[...] = jnp.zeros((components, half), F32)

            high, low = split(rims[stage, h])
            top = 2 * LANES
            rim_operand[0:top, :] = high[:top]
            rim_operand[top : 2 * top, :] = low[:top]
            rim_operand[2 * top : 3 * top, :] = high[:top]
            at = 3 * top
            for m, value in enumerate((high[top:], low[top:], high[top:], jnp.zeros_like(high[top:]))):
                rim_operand[at + m * tail : at + (m + 1) * tail, :] = value
            for f in range(FACES):
                made = jnp.dot(
                    weights[:, f * width : (f + 1) * width], rim_operand[...], preferred_element_type=F32
                )
                high, low = split(made)
                made_high[:, f * HALO : (f + 1) * HALO] = high
                made_low[:, f * HALO : (f + 1) * HALO] = low

            for c in range(chunks):
                here = slice(c * CHUNK, (c + 1) * CHUNK)
                chosen = onehot[h * FACES * HALO : (h + 1) * FACES * HALO, here]
                sum_c = total[c]
                sum_c = sum_c + jnp.dot(made_high[...], chosen, preferred_element_type=F32)
                sum_c = sum_c + jnp.dot(made_low[...], chosen, preferred_element_type=F32)
                if h == 0:
                    total[c] = sum_c
                else:
                    stepped = patched[:, here] + (STEP * jacobian[:, here]) * sum_c
                    if stage == 0:
                        out[:, here] = stepped
                    else:
                        out[:, here] = 0.5 * first[:, here] + 0.5 * stepped

        for j in range(n):
            block_copy(j).wait_send()
        for side in range(2):

            @pl.when(me > 0 if side == 0 else me < n - 1)
            def _():
                for h in range(2):
                    rim_copy(stage, patched, side, h).wait_send()


def local(
    n,
    fields,
    jacobian,
    face_links,
    volume_matrix,
    face_matrices,
    patterns,
    donor_index,
    pattern_index,
    receivers,
):
    components, elements = fields.shape[1:]
    slots = donor_index.shape[1]
    rows = slots // n * 5 // 2
    inner = face_links[0] - HALO
    index = jnp.where((inner >= 0) & (inner < elements), inner, elements) * ROWS
    smem = pl.BlockSpec(memory_space=pltpu.SMEM)
    vmem = pl.BlockSpec(memory_space=pltpu.VMEM)
    hbm = pl.BlockSpec(memory_space=pl.ANY)
    chunks = elements // CHUNK
    width = 8 * LANES
    count = patterns.shape[0]
    result = pl.pallas_call(
        functools.partial(kernel, n),
        out_shape=jax.ShapeDtypeStruct((components, elements), F32),
        in_specs=[smem] + [vmem] * 7 + [hbm] * 2,
        out_specs=vmem,
        scratch_shapes=[
            pltpu.VMEM((components, components), F32),
            pltpu.VMEM((FACES, components, components), F32),
            pltpu.VMEM((components, elements), F32),
            pltpu.VMEM((components, elements), F32),
            pltpu.VMEM((chunks, components, CHUNK), F32),
            pltpu.VMEM((components, 2 * elements), BF16),
            pltpu.VMEM((slots, 2 * elements), BF16),
            pltpu.VMEM((LANES, 3 * count * LANES), BF16),
            pltpu.VMEM((3 * slots, 3 * count * LANES), BF16),
            pltpu.VMEM((slots, 3 * LANES), F32),
            pltpu.VMEM((n * rows, LANES), F32),
            pltpu.VMEM((2, n * rows, LANES), F32),
            pltpu.VMEM((2 * slots, elements), BF16),
            pltpu.VMEM((1, elements), F32),
            pltpu.VMEM((elements * ROWS + 8, LANES), F32),
            pltpu.VMEM((FACES, CHUNK * ROWS, LANES), F32),
            pltpu.VMEM(((FACES + 1) * ROWS, CHUNK, LANES), BF16),
            pltpu.VMEM(((FACES + 1) * ROWS, CHUNK, LANES), BF16),
            pltpu.VMEM((components, (FACES + 1) * width), BF16),
            pltpu.VMEM((2, 2, components, HALO), F32),
            pltpu.VMEM((width, HALO), BF16),
            pltpu.VMEM((components, FACES * HALO), BF16),
            pltpu.VMEM((components, FACES * HALO), BF16),
            pltpu.VMEM((2 * FACES * HALO, elements), BF16),
            pltpu.SemaphoreType.DMA((2, n)),
            pltpu.SemaphoreType.DMA((2, n)),
            pltpu.SemaphoreType.DMA((2, 2, 2)),
            pltpu.SemaphoreType.DMA((2, 2, 2)),
            pltpu.SemaphoreType.DMA((2,)),
        ],
        compiler_params=pltpu.CompilerParams(
            collective_id=0, has_side_effects=True, vmem_limit_bytes=62 * 1024 * 1024
        ),
    )(
        index.reshape(-1),
        fields[0],
        jacobian,
        face_links[0],
        donor_index,
        pattern_index,
        receivers,
        patterns,
        volume_matrix[0],
        face_matrices[0],
    )
    return result[None]


def solution(mesh):
    return jax.shard_map(
        functools.partial(local, mesh.shape["elem"]),
        mesh=mesh,
        in_specs=(
            P("sec", None, "elem"),
            P("sec", "elem"),
            P("sec", None, "elem"),
            P("sec", None, None),
            P("sec", None, None, None),
            P(),
            P("sec", "elem"),
            P("sec", "elem"),
            P("sec", "elem"),
        ),
        out_specs=P("sec", None, "elem"),
        check_vma=False,
    )
```

time: 88.5 us -> 67.8 us (0.77)
  the two profiles are of different devices: /device:TPU:13 before, /device:TPU:1 now
where the time goes in v1:
time: 67.8 us; the launch traced here: 67.5 us
  Pallas kernels  62.2 us (92%)
  local copies, waits for them, and re-layouts  3.88 us (6%)
  other arithmetic  1.36 us (2%)
    pallas_call x1, Pallas kernels, local(): pl.pallas_call(functools.partial(kernel, n), out_shape=jax.ShapeDtypeStru...  62.2 us
    unnamed x2, local copies, waits for them, and re-layouts  3.88 us

profile of v1, /device:TPU:1, one launch (start us, length us, event | category | flops | bytes accessed | tf_op | source)
XLA Modules:
  0.0 67.5 jit_solution(4056832287376238592)
XLA Ops:
  0.0 0.8 %broadcast_add_fusion = s32[1,6,1024]{2,0,1:T(1,128)S(1)} fusion(s32[1,6,1024]{2,0,1:T(1,128)} %param.11), kind=kLoop, calls=%fused_computation.2 | loop fusion | flops 6144 | bytes 49152 | tf_op jit(solution)/shard_map/sub | solution.py:393
  0.8 0.6 select_multiply_fusion.index
  1.4 1.4 %copy.12 = s32[1,6,1024]{2,1,0:T(8,128)} copy(s32[1,6,1024]{2,0,1:T(1,128)} %param.11) | data formatting | bytes 49152
  2.7 62.2 %shard_map.91 = f32[320,1024]{1,0:T(8,128)} custom-call(s32[6144]{0:T(1024)} %select_multiply_fusion.index, f32[320,1024]{1,0:T(8,128)} %bitcast.10, f32[1,1024]{1,0:T(1,128)} %jacobian.1, s32[6,1024]{1,0:T(8,128)} %bitcast.12, s32[1,128]{1,0:T(1,128)} %donors.1, s32[1,128]{1,0:T(1,128)} %choose.1, s32[1,128]{1,0:T(1,128)} %receivers.1, ...), custom_call_target="tpu_custom_call" | custom-call | tf_op jit(solution)/shard_map/pallas_call | solution.py:401
  65.0 2.5 %copy.14 = f32[1,320,1024]{2,1,0:T(8,128)} copy(f32[1,320,1024]{2,1,0:T(8,128)} %bitcast.8) | data formatting | bytes 2621440
